TPU v7x, 256 devices: a whole 4x4x8 slice. The times are simulated.
256 devices in a mesh: row: 16 (over x_lo, y, core), col: 16 (over x_hi, z).
Axes of the slice: x: 4 (x_hi: 2, x_lo: 2; x = x_hi * 2 + x_lo), y: 4, z: 8, core: 2. Of those that a mesh axis runs over, the one named last changes fastest.
Arguments:
- top_inverse: bfloat16 [16, 16, 16, 16, 128, 128], P('row', None, None, 'col'), as said below
- upper_panel: bfloat16 [3, 16, 16, 128, 128], P(None, 'row', 'col'), may hold values from -0.25 to 0.25
- upper_pattern: int32 [3, 16, 16], P(None, 'row', 'col'), may hold values from 0 to 1
- upper_diagonal: float32 [3, 128, 128], replicated, may hold values from -6 to 6
- lower_panel: bfloat16 [8, 16, 16, 128, 128], P(None, 'row', 'col'), may hold values from -0.25 to 0.25
- lower_pattern: int32 [8, 16, 16], P(None, 'row', 'col'), may hold values from 0 to 1, as said below
- parents: int32 [8], replicated, may hold values from 0 to 2, as said below
- parent_panel: bfloat16 [8, 128, 128], replicated, may hold values from -0.5 to 0.5
- lower_diagonal: float32 [8, 128, 128], replicated, may hold values from -6 to 6
Outputs:
- upper_columns: bfloat16 [3, 16, 16, 128, 128], P(None, 'row', 'col')
- upper_blocks: float32 [3, 128, 128], replicated
- lower_columns: bfloat16 [8, 16, 16, 128, 128], P(None, 'row', 'col')
- lower_cross: float32 [8, 128, 128], replicated
- lower_blocks: float32 [8, 128, 128], replicated
Inputs may be any that keep to these rules, and one draw needn't show every extreme that they name: top_inverse is symmetric: block (I, J) is the transpose of block (J, I). `lower_pattern`: A second-level pattern is zero wherever the pattern of its parent is zero. `parents`: every first-level supernode is the parent of some second-level supernode.
All inputs are finite; a program needn't handle non-finite values.
Results may differ from a plain program's by a relative error of at most 0.0041.
Values may be sent and summed in bfloat16 or wider, within the bound.
A program may use at most 128 MiB of HBM per device.

v0:
```python
import jax
import jax.numpy as jnp
from jax import lax
from jax.sharding import PartitionSpec as P

HIGH = lax.Precision.HIGHEST


def by_rows(top_inverse, panel):
    partial_value = jnp.einsum(
        "aibjxy,kbjyz->iakxz",
        top_inverse,
        lax.all_gather(panel, "row", axis=1, tiled=True),
        preferred_element_type=jnp.float32,
    )
    reduced = lax.psum_scatter(partial_value, "col", scatter_dimension=0, tiled=True)
    return jnp.transpose(reduced, (2, 1, 0, 3, 4))


def upper_part(upper_product, upper_mask, upper_masked, lower_masked, parents):
    upper_columns = (-upper_product * upper_mask).astype(jnp.bfloat16)
    selected = jnp.take(upper_columns, parents, axis=0)
    local_upper = jnp.einsum(
        "ktsxy,ktsxz->kyz", upper_masked, upper_columns, preferred_element_type=jnp.float32
    )
    local_cross = jnp.einsum(
        "mtsxy,mtsxz->myz", selected, lower_masked, preferred_element_type=jnp.float32
    )
    return (upper_columns, selected, local_upper, local_cross)


def lower_part(lower_product, selected, parent_panel, lower_mask, lower_masked):
    extension = jnp.einsum(
        "mtsxy,myz->mtsxz", selected, parent_panel, preferred_element_type=jnp.float32
    )
    lower_columns = (-(lower_product + extension) * lower_mask).astype(jnp.bfloat16)
    local_lower = jnp.einsum(
        "mtsxy,mtsxz->myz", lower_masked, lower_columns, preferred_element_type=jnp.float32
    )
    return (lower_columns, local_lower)


def per_device(
    top_inverse,
    upper_panel,
    upper_pattern,
    upper_diagonal,
    lower_panel,
    lower_pattern,
    parents,
    parent_panel,
    lower_diagonal,
):
    upper_mask = upper_pattern.astype(jnp.float32)[:, :, :, None, None]
    upper_masked = upper_panel * upper_mask.astype(jnp.bfloat16)
    lower_mask = lower_pattern.astype(jnp.float32)[:, :, :, None, None]
    lower_masked = lower_panel * lower_mask.astype(jnp.bfloat16)
    upper_product = by_rows(top_inverse, upper_masked)
    upper_columns, selected, local_upper, local_cross = upper_part(
        upper_product, upper_mask, upper_masked, lower_masked, parents
    )
    summed_upper, summed_cross = lax.psum((local_upper, local_cross), ("row", "col"))
    lower_product = by_rows(top_inverse, lower_masked)
    lower_columns, local_lower = lower_part(
        lower_product, selected, parent_panel, lower_mask, lower_masked
    )
    summed_lower = lax.psum(local_lower, ("row", "col"))
    upper_blocks = upper_diagonal - summed_upper
    panel_wide = parent_panel.astype(jnp.float32)
    parent_blocks = jnp.take(upper_blocks, parents, axis=0)
    lower_cross = -summed_cross - jnp.einsum(
        "mxy,myz->mxz", parent_blocks, panel_wide, precision=HIGH
    )
    lower_blocks = (
        lower_diagonal
        - summed_lower
        - jnp.einsum("myx,myz->mxz", panel_wide, lower_cross, precision=HIGH)
    )
    return (upper_columns, upper_blocks, lower_columns, lower_cross, lower_blocks)


def solution(mesh):
    return jax.shard_map(
        per_device,
        mesh=mesh,
        in_specs=(
            P("row", None, None, "col", None, None),
            P(None, "row", "col", None, None),
            P(None, "row", "col"),
            P(),
            P(None, "row", "col", None, None),
            P(None, "row", "col"),
            P(),
            P(),
            P(),
        ),
        out_specs=(
            P(None, "row", "col", None, None),
            P(),
            P(None, "row", "col", None, None),
            P(),
            P(),
        ),
        check_vma=False,
    )
```

profile of v0, /device:TPU:8, one launch (start us, length us, event | category | flops | bytes accessed | tf_op | source)
XLA Modules:
  0.0 649.7 jit_solution(10669901075646859960)
XLA Ops:
  7.2 0.0 all-gather.3.cloned.1.call-start
  7.2 0.7 fusion.31
  7.9 1.0 copy.49
  8.9 0.7 broadcast_multiply_fusion.1
  9.7 0.0 all-gather.5.cloned.1.call-start
  9.7 1.1 copy.51
  10.9 0.7 convert_bitcast_fusion
  11.5 0.8 broadcast_multiply_fusion
  12.3 0.0 all-reduce.9.cloned.1.call-start
  12.4 36.1 %all-gather.3.cloned.1.call-done = bf16[3,16,1,128,128]{3,4,1,0,2:T(8,128)(2,1)} async-done(((bf16[3,1,1,128,128]{3,4,1,0,2:T(8,128)(2,1)}), bf16[3,16,1,128,128]{3,4,1,0,2:T(8,128)(2,1)}) %all-gather.3.cloned.1.call-update) | async-done | bytes 1572880 | tf_op jit(solution)/shard_map/all_gather | solution.py:13
  48.5 7.5 %fusion.10 = f32[16,1,3,128,128]{3,4,0,2,1:T(8,128)} fusion(bf16[1,16,16,1,128,128]{5,4,3,2,1,0:T(8,128)(2,1)} %param.9, bf16[3,16,1,128,128]{3,4,1,0,2:T(8,128)(2,1)} %all-gather.3.cloned.1.call-done), kind=kOutput, calls=%fused_computation.8 | convolution fusion | flops 3221225472 | bytes 13107200 | tf_op jit(solution)/shard_map/aibjxy,kbjyz->iakxz/dot_general | solution.py:10
  55.9 34.7 %all-gather.5.cloned.1.call-done = bf16[8,16,1,128,128]{3,4,1,0,2:T(8,128)(2,1)} async-done(((bf16[8,1,1,128,128]{3,4,1,0,2:T(8,128)(2,1)}), bf16[8,16,1,128,128]{3,4,1,0,2:T(8,128)(2,1)}) %all-gather.5.cloned.1.call-update) | async-done | bytes 4194320 | tf_op jit(solution)/shard_map/all_gather | solution.py:13
  90.6 13.6 %fusion.5 = f32[16,1,8,128,128]{3,4,0,2,1:T(8,128)} fusion(bf16[1,16,16,1,128,128]{5,4,3,2,1,0:T(8,128)(2,1)} %param.9, bf16[8,16,1,128,128]{3,4,1,0,2:T(8,128)(2,1)} %all-gather.5.cloned.1.call-done), kind=kOutput, calls=%fused_computation.7 | convolution fusion | flops 8589934592 | bytes 20971520 | tf_op jit(solution)/shard_map/aibjxy,kbjyz->iakxz/dot_general | solution.py:10
  104.3 0.0 all-reduce.7.cloned.1.call-start
  104.3 0.6 copy-done.9
  104.9 0.6 dynamic-slice
  105.5 264.7 %all-reduce.9.cloned.1.call-done = (f32[16,1,3,128,128]{3,4,0,2,1:T(8,128)}, f32[16,1,8,128,128]{3,4,0,2,1:T(8,128)}) async-done(((f32[16,1,3,128,128]{3,4,0,2,1:T(8,128)}, f32[16,1,8,128,128]{3,4,0,2,1:T(8,128)}), (f32[16,1,3,128,128]{3,4,0,2,1:T(8,128)}, f32[16,1,8,128,128]{3,4,0,2,1:T(8,128)})) %all-reduce.9.cloned.1.call-update) | async-done | bytes 11534352
  370.2 1.6 constant_dynamic-slice_fusion.1
  371.8 0.1 copy.50
  371.9 0.7 fusion.37
  372.7 0.9 fusion.27
  373.6 1.7 constant_dynamic-slice_fusion
  375.3 0.2 copy.52
  375.5 0.6 gather_fusion
  376.2 1.2 fusion.21
  377.4 0.3 fusion.17
  377.7 1.0 fusion.19
  378.7 258.8 %all-reduce.7.cloned.1.call-done = (f32[3,128,128]{2,1,0:T(8,128)}, f32[8,128,128]{2,1,0:T(8,128)}, f32[8,128,128]{2,1,0:T(8,128)}) async-done(((f32[3,128,128]{2,1,0:T(8,128)}, f32[8,128,128]{2,1,0:T(8,128)}, f32[8,128,128]{2,1,0:T(8,128)}), (f32[3,128,128]{2,1,0:T(8,128)}, f32[8,128,128]{2,1,0:T(8,128)}, f32[8,128,128]{2,1,0:T(8,128)})) %all-reduce.7.cloned.1.call-update) | async-done | bytes 1245200 | tf_op jit(solution)/shard_map/psum | solution.py:62
  637.5 0.9 sub.12
  638.5 0.6 gather_fusion.1
  639.1 1.5 convolution_subtract_fusion
  640.6 2.5 fusion.16
  (26 shorter events, 0.1 us)
Async XLA Ops:
  7.2 370.2 %copy-start = (bf16[8,128,128]{2,1,0:T(8,128)(2,1)S(1)}, bf16[8,128,128]{2,1,0:T(8,128)(2,1)}, u32[]{:S(2)}) copy-start(bf16[8,128,128]{2,1,0:T(8,128)(2,1)} %param.16) | copy-start | bytes 786436
  7.2 41.3 %all-gather.3.cloned.1.call-start = ((), (), s32[]{:S(2)}) async-start(), calls=%async_computation | async-start | bytes 1671168 | tf_op jit(solution)/shard_map/all_gather | solution.py:13
  9.7 80.9 %all-gather.5.cloned.1.call-start = ((), (), s32[]{:S(2)}) async-start(), calls=%async_computation.1 | async-start | bytes 4456448 | tf_op jit(solution)/shard_map/all_gather | solution.py:13
  12.3 357.9 %all-reduce.9.cloned.1.call-start = ((), (), s32[]{:S(2)}) async-start(), calls=%async_computation.3 | async-start | bytes 23068672
  104.2 0.7 copy-start.9
  104.2 1.3 copy-start.8
  104.2 268.5 %copy-start.5 = (bf16[3,1,1,128,128]{3,4,1,0,2:T(8,128)(2,1)S(1)}, bf16[3,1,1,128,128]{3,4,1,0,2:T(8,128)(2,1)}, u32[]{:S(2)}) copy-start(bf16[3,1,1,128,128]{3,4,1,0,2:T(8,128)(2,1)} %broadcast_multiply_fusion.1) | copy-start | bytes 294916
  104.3 271.9 %copy-start.1 = (bf16[8,1,1,128,128]{3,4,1,0,2:T(8,128)(2,1)S(1)}, bf16[8,1,1,128,128]{3,4,1,0,2:T(8,128)(2,1)}, u32[]{:S(2)}) copy-start(bf16[8,1,1,128,128]{3,4,1,0,2:T(8,128)(2,1)} %broadcast_multiply_fusion) | copy-start | bytes 786436
  104.3 533.2 %all-reduce.7.cloned.1.call-start = ((), (), s32[]{:S(2)}) async-start(), calls=%async_computation.2 | async-start | bytes 2490368 | tf_op jit(solution)/shard_map/psum | solution.py:62
  371.8 265.7 %copy-start.7 = (f32[3,128,128]{2,1,0:T(8,128)S(1)}, f32[3,128,128]{2,1,0:T(8,128)}, u32[]{:S(2)}) copy-start(f32[3,128,128]{2,1,0:T(8,128)} %param.12) | copy-start | bytes 589828
  376.2 264.4 %copy-start.6 = (f32[8,128,128]{2,1,0:T(8,128)S(1)}, f32[8,128,128]{2,1,0:T(8,128)}, u32[]{:S(2)}) copy-start(f32[8,128,128]{2,1,0:T(8,128)} %param.17) | copy-start | bytes 1572868
  377.7 265.4 %copy-start.4 = (bf16[8,128,128]{2,1,0:T(8,128)(2,1)}, bf16[8,128,128]{2,1,0:T(8,128)(2,1)S(1)}, u32[]{:S(2)}) copy-start(bf16[8,128,128]{2,1,0:T(8,128)(2,1)S(1)} %fusion.17) | copy-start | bytes 786436
  638.5 4.6 copy-start.2
  640.6 2.5 copy-start.3
Sparse Core Ops, SparseCore 0:
  10.4 38.0 all-gather.2
  50.8 39.7 all-gather.4
  104.4 265.7 all-reduce.8
  378.9 258.6 all-reduce.6
where the time goes:
time: 650 us
  waiting for transfers between devices  594 us (91%)
  matrix products  28.5 us (4%)
  between operations  13.9 us (2%)
  local copies, waits for them, and re-layouts  8.16 us (1%)
    unnamed x5, waiting for transfers between devices  265 us
    psum x1, waiting for transfers between devices, per_device(): lax.psum((local_upper, local_cross), ('row', 'col'))  259 us
    all_gather x2, waiting for transfers between devices, by_rows(): lax.all_gather(panel, 'row', axis=1, tiled=True)  70.7 us
    dot_general x2, matrix products, by_rows(): jnp.einsum('aibjxy,kbjyz->iakxz', top_inverse, lax.all_gather(panel, 'row...  21.1 us
  transfers between devices with their start and end apart: 4, of which 4 were waited for; matrix products, arithmetic and copies ran while one was open for 2% of the time, Pallas kernels for 0%

commit v1 on v0

--- a/solution.py
+++ b/solution.py
@@ -59,7 +59,7 @@
     upper_columns, selected, local_upper, local_cross = upper_part(
         upper_product, upper_mask, upper_masked, lower_masked, parents
     )
-    summed_upper, summed_cross = lax.psum((local_upper, local_cross), ("row", "col"))
+    summed_upper, summed_cross = lax.psum(lax.psum((local_upper, local_cross), "row"), "col")
     lower_product = by_rows(top_inverse, lower_masked)
     lower_columns, local_lower = lower_part(
         lower_product, selected, parent_panel, lower_mask, lower_masked

time: 650 us -> 880 us (1.35)
  waiting for transfers between devices: 594 us -> 825 us
    psum x1 -> x3, waiting for transfers between devices: 259 us -> 587 us  [the longest x1 251 us: per_device(): summed_lower = lax.psum(local_lower, ('row', 'col'))]
    unnamed x5 -> x7, waiting for transfers between devices: 265 us -> 167 us
  transfers between devices with their start and end apart: 4 -> 6, of which waited for: 4 -> 6; matrix products, arithmetic and copies ran while one was open for 2% -> 3% of each run, Pallas kernels for 0% -> 0%
where the time goes in v1:
time: 880 us
  waiting for transfers between devices  825 us (94%)
  matrix products  29.3 us (3%)
  between operations  14.3 us (2%)
    psum x1, waiting for transfers between devices, per_device(): summed_lower = lax.psum(local_lower, ('row', 'col'))  251 us
    psum x1, waiting for transfers between devices, per_device(): lax.psum(lax.psum((local_upper, local_cross), 'row'), 'col')  225 us
    unnamed x7, waiting for transfers between devices  167 us
    psum x1, waiting for transfers between devices, per_device(): lax.psum((local_upper, local_cross), 'row')  111 us
    all_gather x2, waiting for transfers between devices, by_rows(): lax.all_gather(panel, 'row', axis=1, tiled=True)  71 us
    dot_general x2, matrix products, by_rows(): jnp.einsum('aibjxy,kbjyz->iakxz', top_inverse, lax.all_gather(panel, 'row...  21.1 us
  transfers between devices with their start and end apart: 6, of which 6 were waited for; matrix products, arithmetic and copies ran while one was open for 3% of the time, Pallas kernels for 0%

profile of v1, /device:TPU:8, one launch (start us, length us, event | category | flops | bytes accessed | tf_op | source)
XLA Modules:
  0.0 879.6 jit_solution(14832193262104455089)
XLA Ops:
  7.2 0.7 fusion.31
  7.9 1.0 copy.49
  8.9 0.7 broadcast_multiply_fusion.1
  9.7 0.0 all-reduce.11.cloned.1.call-start
  9.8 38.7 %all-gather.3.cloned.1.call-done = bf16[3,16,1,128,128]{3,4,1,0,2:T(8,128)(2,1)} async-done(((bf16[3,1,1,128,128]{3,4,1,0,2:T(8,128)(2,1)}), bf16[3,16,1,128,128]{3,4,1,0,2:T(8,128)(2,1)}) %all-gather.3.cloned.1.call-update) | async-done | bytes 1572880 | tf_op jit(solution)/shard_map/all_gather | solution.py:13
  48.5 7.5 fusion.10
  56.0 0.0 all-gather.5.cloned.1.call-start
  56.0 0.2 copy.51
  56.2 0.8 broadcast_multiply_fusion
  57.0 0.0 all-reduce.15.cloned.1.call-start
  57.1 0.6 dynamic-slice
  57.7 166.9 %all-reduce.11.cloned.1.call-done = f32[16,1,3,128,128]{3,4,0,2,1:T(8,128)} async-done(((f32[16,1,3,128,128]{3,4,0,2,1:T(8,128)}), f32[16,1,3,128,128]{3,4,0,2,1:T(8,128)}) %all-reduce.11.cloned.1.call-update) | async-done | bytes 3145744
  224.6 1.6 constant_dynamic-slice_fusion.1
  226.2 0.1 copy.50
  226.4 0.7 fusion.37
  227.1 0.6 gather_fusion
  227.7 0.9 fusion.27
  228.6 2.2 fusion.21
  230.8 0.0 all-reduce.13.cloned.1.call-start
  230.9 32.3 %all-gather.5.cloned.1.call-done = bf16[8,16,1,128,128]{3,4,1,0,2:T(8,128)(2,1)} async-done(((bf16[8,1,1,128,128]{3,4,1,0,2:T(8,128)(2,1)}), bf16[8,16,1,128,128]{3,4,1,0,2:T(8,128)(2,1)}) %all-gather.5.cloned.1.call-update) | async-done | bytes 4194320 | tf_op jit(solution)/shard_map/all_gather | solution.py:13
  263.2 13.6 %fusion.5 = f32[16,1,8,128,128]{3,4,0,2,1:T(8,128)} fusion(bf16[1,16,16,1,128,128]{5,4,3,2,1,0:T(8,128)(2,1)} %param.9, bf16[8,16,1,128,128]{3,4,1,0,2:T(8,128)(2,1)} %all-gather.5.cloned.1.call-done), kind=kOutput, calls=%fused_computation.7 | convolution fusion | flops 8589934592 | bytes 20971520 | tf_op jit(solution)/shard_map/aibjxy,kbjyz->iakxz/dot_general | solution.py:10
  276.8 111.3 %all-reduce.15.cloned.1.call-done = (f32[3,128,128]{2,1,0:T(8,128)}, f32[8,128,128]{2,1,0:T(8,128)}) async-done(((f32[3,128,128]{2,1,0:T(8,128)}, f32[8,128,128]{2,1,0:T(8,128)}), (f32[3,128,128]{2,1,0:T(8,128)}, f32[8,128,128]{2,1,0:T(8,128)})) %all-reduce.15.cloned.1.call-update) | async-done | bytes 720912 | tf_op jit(solution)/shard_map/psum | solution.py:62
  388.2 224.8 %all-reduce.13.cloned.1.call-done = (f32[3,128,128]{2,1,0:T(8,128)}, f32[16,1,8,128,128]{3,4,0,2,1:T(8,128)}, f32[8,128,128]{2,1,0:T(8,128)}) async-done(((f32[3,128,128]{2,1,0:T(8,128)}, f32[16,1,8,128,128]{3,4,0,2,1:T(8,128)}, f32[8,128,128]{2,1,0:T(8,128)}), (f32[3,128,128]{2,1,0:T(8,128)}, f32[16,1,8,128,128]{3,4,0,2,1:T(8,128)}, f32[8,128,128]{2,1,0:T(8,128)})) %all-reduce.13.cloned.1.call-update) | async-done | bytes 9109520 | tf_op jit(solution)/shard_map/psum | solution.py:62
  613.0 1.0 sub.12
  614.1 0.6 gather_fusion.1
  614.6 1.7 constant_dynamic-slice_fusion
  616.4 0.2 copy.52
  616.6 0.3 fusion.17
  616.9 1.0 fusion.19
  617.9 1.5 convolution_subtract_fusion
  619.5 251.0 %all-reduce.9.cloned.1.call-done = f32[8,128,128]{2,1,0:T(8,128)} async-done(((f32[8,128,128]{2,1,0:T(8,128)}), f32[8,128,128]{2,1,0:T(8,128)}) %all-reduce.9.cloned.1.call-update) | async-done | bytes 524304 | tf_op jit(solution)/shard_map/psum | solution.py:67
  870.4 2.3 fusion.16
  (36 shorter events, 0.3 us)
Async XLA Ops:
  7.2 609.4 %copy-start = (bf16[8,128,128]{2,1,0:T(8,128)(2,1)S(1)}, bf16[8,128,128]{2,1,0:T(8,128)(2,1)}, u32[]{:S(2)}) copy-start(bf16[8,128,128]{2,1,0:T(8,128)(2,1)} %param.16) | copy-start | bytes 786436
  7.2 41.3 %all-gather.3.cloned.1.call-start = ((), (), s32[]{:S(2)}) async-start(), calls=%async_computation | async-start | bytes 1671168 | tf_op jit(solution)/shard_map/all_gather | solution.py:13
  9.7 46.3 %copy-start.7 = (bf16[8,1,1,128,128]{4,3,2,1,0:T(8,128)(2,1)S(1)}, bf16[8,1,1,128,128]{4,3,2,1,0:T(8,128)(2,1)}, u32[]{:S(2)}) copy-start(bf16[8,1,1,128,128]{4,3,2,1,0:T(8,128)(2,1)} %param.13) | copy-start | bytes 786436
  9.7 46.5 %copy-start.9 = (s32[8,1,1]{0,2,1:T(1,128)S(1)}, s32[8,1,1]{0,2,1:T(1,128)}, u32[]{:S(2)}) copy-start(s32[8,1,1]{0,2,1:T(1,128)} %param.14) | copy-start | bytes 100
  9.7 214.9 %all-reduce.11.cloned.1.call-start = ((), (), s32[]{:S(2)}) async-start(), calls=%async_computation.3 | async-start | bytes 6291456
  55.9 1.2 copy-start.11
  55.9 1.8 copy-start.10
  55.9 171.8 %copy-start.5 = (bf16[3,1,1,128,128]{3,4,1,0,2:T(8,128)(2,1)S(1)}, bf16[3,1,1,128,128]{3,4,1,0,2:T(8,128)(2,1)}, u32[]{:S(2)}) copy-start(bf16[3,1,1,128,128]{3,4,1,0,2:T(8,128)(2,1)} %broadcast_multiply_fusion.1) | copy-start | bytes 294916
  56.0 207.2 %all-gather.5.cloned.1.call-start = ((), (), s32[]{:S(2)}) async-start(), calls=%async_computation.1 | async-start | bytes 4456448 | tf_op jit(solution)/shard_map/all_gather | solution.py:13
  57.0 331.1 %all-reduce.15.cloned.1.call-start = ((), (), s32[]{:S(2)}) async-start(), calls=%async_computation.5 | async-start | bytes 1441792 | tf_op jit(solution)/shard_map/psum | solution.py:62
  230.8 382.2 %all-reduce.13.cloned.1.call-start = ((), (), s32[]{:S(2)}) async-start(), calls=%async_computation.4 | async-start | bytes 18219008 | tf_op jit(solution)/shard_map/psum | solution.py:62
  388.1 224.9 %copy-start.8 = (f32[3,128,128]{2,1,0:T(8,128)S(1)}, f32[3,128,128]{2,1,0:T(8,128)}, u32[]{:S(2)}) copy-start(f32[3,128,128]{2,1,0:T(8,128)} %param.12) | copy-start | bytes 589828
  388.1 228.8 %copy-start.1 = (bf16[8,1,1,128,128]{3,4,1,0,2:T(8,128)(2,1)S(1)}, bf16[8,1,1,128,128]{3,4,1,0,2:T(8,128)(2,1)}, u32[]{:S(2)}) copy-start(bf16[8,1,1,128,128]{3,4,1,0,2:T(8,128)(2,1)} %broadcast_multiply_fusion) | copy-start | bytes 786436
  388.1 482.3 %all-reduce.9.cloned.1.call-start = ((), (), s32[]{:S(2)}) async-start(), calls=%async_computation.2 | async-start | bytes 1048576 | tf_op jit(solution)/shard_map/psum | solution.py:67
  613.0 257.4 %copy-start.6 = (f32[8,128,128]{2,1,0:T(8,128)S(1)}, f32[8,128,128]{2,1,0:T(8,128)}, u32[]{:S(2)}) copy-start(f32[8,128,128]{2,1,0:T(8,128)} %param.17) | copy-start | bytes 1572868
  614.0 258.7 %copy-start.2 = (f32[3,128,128]{2,1,0:T(8,128)}, f32[3,128,128]{2,1,0:T(8,128)S(1)}, u32[]{:S(2)}) copy-start(f32[3,128,128]{2,1,0:T(8,128)S(1)} %sub.12) | copy-start | bytes 589828
  616.9 255.8 %copy-start.4 = (bf16[8,128,128]{2,1,0:T(8,128)(2,1)}, bf16[8,128,128]{2,1,0:T(8,128)(2,1)S(1)}, u32[]{:S(2)}) copy-start(bf16[8,128,128]{2,1,0:T(8,128)(2,1)S(1)} %fusion.17) | copy-start | bytes 786436
  619.4 253.3 %copy-start.3 = (f32[8,128,128]{2,1,0:T(8,128)}, f32[8,128,128]{2,1,0:T(8,128)S(1)}, u32[]{:S(2)}) copy-start(f32[8,128,128]{2,1,0:T(8,128)S(1)} %convolution_subtract_fusion) | copy-start | bytes 1572868
Sparse Core Ops, SparseCore 0:
  10.4 38.0 all-gather.2
  56.1 168.5 all-reduce.10
  227.0 36.0 all-gather.4
  266.3 121.7 all-reduce.14
  390.9 222.1 all-reduce.12
  618.9 251.4 all-reduce.8
